TPU v7x, 32 devices: a whole 2x2x4 slice. The times are simulated.
32 devices in a mesh: op: 4 (over y, x), str: 8 (over z, core).
Axes of the slice: x: 2, y: 2, z: 4, core: 2. Of those that a mesh axis runs over, the one named last changes fastest.
Arguments:
- coeffs: float32 [4096, 4096], P('str'), may hold values from -6 to 6
- previous: float32 [4096, 4096], P('str'), may hold values from -6 to 6
- block_values: bfloat16 [4, 32, 6, 128, 128], P('op'), may hold values from -0.21875 to 0.21875
- block_cols: int32 [4, 32, 6], P('op'), may hold values from 0 to 31, as said below
Outputs:
- advanced: float32 [4096, 4096], P('str')
Inputs may be any that keep to these rules, and one draw needn't show every extreme that they name: For every term k and block row r, block_cols[k, r, 0] equals r and the 6 entries of block_cols[k, r] are distinct.
All inputs are finite; a program needn't handle non-finite values.
Results may differ from a plain program's by a relative error of at most 0.0003.
Values sent between devices are 32-bit elements; how exact they have to be, the bound alone decides.
A program may use at most 192 MiB of HBM per device.

v0:
```python
import math

import jax
import jax.numpy as jnp
from jax import lax
from jax.sharding import PartitionSpec as P

STEPS = 2


def per_device(coeffs, previous, block_values, block_cols):
    local_terms = block_values.shape[0]
    step_scale = 2.0 / math.sqrt(local_terms * lax.axis_size("op"))
    factors = block_values.astype(jnp.float32)
    row_count, full_width = coeffs.shape
    block_size = block_values.shape[-1]
    block_count = full_width // block_size
    slot_count = block_cols.shape[2]
    regrouped = lax.all_to_all(
        previous.reshape(row_count, block_count, block_size),
        "str",
        split_axis=1,
        concat_axis=0,
        tiled=True,
    )
    earlier = regrouped.reshape(full_width, row_count).T
    current = coeffs
    for step_index in range(STEPS):
        column_list = block_cols[0].reshape(-1)
        term_factors = factors[0]
        gathered = jnp.take(
            current.reshape(row_count, block_count, block_size), column_list, axis=1
        )
        gathered = gathered.reshape(row_count, block_count, slot_count, block_size)
        beta_side = jnp.einsum(
            "arjc,rjoc->aro", gathered, term_factors, precision=lax.Precision.HIGHEST
        )
        received = lax.all_to_all(beta_side, "str", split_axis=1, concat_axis=0, tiled=True)
        group_count = received.shape[1]
        item_count = received.shape[2]
        grouped = jnp.take(
            received.reshape(block_count, block_size, group_count, item_count), column_list, axis=0
        )
        grouped = grouped.reshape(block_count, slot_count, block_size, group_count, item_count)
        result = jnp.einsum(
            "rjoc,rjcnm->nmro", term_factors, grouped, precision=lax.Precision.HIGHEST
        )
        moved = result.reshape(group_count, item_count, full_width)
        summed = moved.reshape(row_count, full_width)
        updated = step_scale * lax.psum(summed, "op") - earlier
        earlier, current = (current, updated)
    return current


def solution(mesh):
    placed = (P("str", None), P("str", None), P("op", None, None, None, None), P("op", None, None))
    return jax.shard_map(
        per_device, mesh=mesh, in_specs=placed, out_specs=P("str", None), check_vma=False
    )
```

profile of v0, /device:TPU:0, one launch (start us, length us, event | category | flops | bytes accessed | tf_op | source)
XLA Modules:
  0.0 1236.2 jit_solution(6269851794979325475)
XLA Ops:
  6.5 0.8 copy.25
  7.3 0.1 reshape_squeeze.4
  7.4 9.0 copy.26
  16.4 9.0 copy.27
  25.3 22.2 %gather_fusion = f32[192,512,128]{2,1,0:T(8,128)} fusion(f32[512,32,128]{2,0,1:T(8,128)} %copy.27, s32[1024]{0:T(1024)S(1)} %pad_clamp_fusion), kind=kCustom, calls=%fused_computation.clone | custom fusion | bytes 100664064 | tf_op jit(solution)/shard_map/jit(_take)/gather | solution.py:31
  47.6 34.0 %broadcast_select_fusion.3 = f32[192,512,128]{2,1,0:T(8,128)} fusion(f32[192,512,128]{2,1,0:T(8,128)} %gather_fusion, pred[192]{0:T(512)(128)(4,1)S(1)} %compare_and_fusion), kind=kLoop, calls=%fused_computation.7 | loop fusion | flops 12582912 | bytes 100663488 | tf_op jit(solution)/shard_map/jit(_take)/select_n | solution.py:31
  81.6 30.1 %fusion.8 = f32[512,32,128]{2,0,1:T(8,128)} fusion(f32[512,32,6,128]{3,0,2,1:T(8,128)} %bitcast.92, bf16[1,32,6,128,128]{4,3,2,1,0:T(8,128)(2,1)} %param.10), kind=kOutput, calls=%fused_computation.19 | convolution fusion | flops 19327352832 | bytes 65011712 | tf_op jit(solution)/shard_map/arjc,rjoc->aro/dot_general | solution.py:35
  111.7 6.4 all-to-all-start
  118.1 9.0 copy.31
  127.1 175.0 %all-to-all-done = f32[512,32,128]{2,0,1:T(8,128)} async-done(((f32[512,32,128]{2,0,1:T(8,128)}), f32[512,32,128]{2,0,1:T(8,128)}, u32[]{:S(2)}, u32[]{:S(2)}) %all-to-all-start) | async-done | bytes 8388640 | tf_op jit(solution)/shard_map/all_to_all | solution.py:38
  302.0 4.9 all-to-all-start.1
  307.0 0.0 all-reduce.3.cloned.1.call-start
  307.0 7.7 copy.28
  314.7 22.2 %gather_fusion.1 = f32[192,128,4,128]{3,1,2,0:T(8,128)} fusion(f32[32,128,4,128]{3,1,0,2:T(8,128)} %bitcast.91, s32[1024]{0:T(1024)S(1)} %pad_clamp_fusion), kind=kCustom, calls=%fused_computation.1.clone | custom fusion | bytes 100664064 | tf_op jit(solution)/shard_map/jit(_take)/gather | solution.py:41
  336.9 34.9 %broadcast_select_fusion.1 = f32[192,128,4,128]{3,1,2,0:T(8,128)} fusion(f32[192,128,4,128]{3,1,2,0:T(8,128)} %gather_fusion.1, pred[192]{0:T(512)(128)(4,1)S(1)} %compare_and_fusion), kind=kLoop, calls=%fused_computation.5 | loop fusion | flops 12582912 | bytes 100663488 | tf_op jit(solution)/shard_map/jit(_take)/select_n | solution.py:41
  371.9 48.2 %fusion.14 = f32[4,128,32,128]{3,1,0,2:T(8,128)} fusion(f32[32,6,128,4,128]{4,2,3,1,0:T(8,128)} %bitcast.95, bf16[1,32,6,128,128]{4,3,2,1,0:T(8,128)(2,1)} %param.10), kind=kOutput, calls=%fused_computation.21 | convolution fusion | flops 19327352832 | bytes 65011712 | tf_op jit(solution)/shard_map/rjoc,rjcnm->nmro/dot_general | solution.py:45
  420.1 8.2 copy.30
  428.3 11.7 copy.55
  440.0 0.0 all-reduce.3.cloned.1.call-update
  440.1 0.0 all-reduce.5.cloned.1.call-start
  440.1 50.7 %all-to-all-done.1 = f32[512,32,128]{0,2,1:T(8,128)} async-done(((f32[512,32,128]{0,2,1:T(8,128)}), f32[512,32,128]{0,2,1:T(8,128)}, u32[]{:S(2)}, u32[]{:S(2)}) %all-to-all-start.1) | async-done | bytes 8388640 | tf_op jit(solution)/shard_map/all_to_all | solution.py:19
  490.8 8.4 copy.33
  499.2 11.7 copy.50
  510.9 102.6 %all-reduce.3.cloned.1.call-done = f32[512,4096]{1,0:T(8,128)} async-done(((f32[512,4096]{1,0:T(8,128)}), f32[512,4096]{1,0:T(8,128)}) %all-reduce.3.cloned.1.call-update) | async-done | bytes 8388624 | tf_op jit(solution)/shard_map/psum | solution.py:50
  613.6 11.3 bitcast_subtract_fusion
  624.9 9.0 copy.34
  633.9 8.9 copy.35
  642.8 22.2 %gather_fusion.2 = f32[192,512,128]{2,1,0:T(8,128)} fusion(f32[512,32,128]{2,0,1:T(8,128)} %copy.35, s32[1024]{0:T(1024)S(1)} %pad_clamp_fusion), kind=kCustom, calls=%fused_computation.2.clone | custom fusion | bytes 100664064 | tf_op jit(solution)/shard_map/jit(_take)/gather | solution.py:31
  665.0 34.0 %broadcast_select_fusion.2 = f32[192,512,128]{2,1,0:T(8,128)} fusion(f32[192,512,128]{2,1,0:T(8,128)} %gather_fusion.2, pred[192]{0:T(512)(128)(4,1)S(1)} %compare_and_fusion), kind=kLoop, calls=%fused_computation.6 | loop fusion | flops 12582912 | bytes 100663488 | tf_op jit(solution)/shard_map/jit(_take)/select_n | solution.py:31
  699.1 30.1 %fusion.11 = f32[512,32,128]{2,0,1:T(8,128)} fusion(f32[512,32,6,128]{3,0,2,1:T(8,128)} %bitcast.93, bf16[1,32,6,128,128]{4,3,2,1,0:T(8,128)(2,1)} %param.10), kind=kOutput, calls=%fused_computation.20 | convolution fusion | flops 19327352832 | bytes 65011712 | tf_op jit(solution)/shard_map/arjc,rjoc->aro/dot_general | solution.py:35
  729.2 189.0 %all_to_all.45 = f32[512,32,128]{2,0,1:T(8,128)S(1)} all-to-all(f32[512,32,128]{2,0,1:T(8,128)} %fusion.11), channel_id=1, replica_groups=mesh['op'=4,'str'=8] {'str'}, dimensions={1} | all-to-all | bytes 16777216 | tf_op jit(solution)/shard_map/all_to_all | solution.py:38
  918.1 4.0 copy.36
  922.1 22.2 %gather_fusion.3 = f32[192,128,4,128]{3,1,2,0:T(8,128)} fusion(f32[32,128,4,128]{3,1,0,2:T(8,128)} %bitcast.90, s32[1024]{0:T(1024)S(1)} %pad_clamp_fusion), kind=kCustom, calls=%fused_computation.3.clone | custom fusion | bytes 100664064 | tf_op jit(solution)/shard_map/jit(_take)/gather | solution.py:41
  944.3 34.9 %broadcast_select_fusion = f32[192,128,4,128]{3,1,2,0:T(8,128)} fusion(f32[192,128,4,128]{3,1,2,0:T(8,128)} %gather_fusion.3, pred[192]{0:T(512)(128)(4,1)S(1)} %compare_and_fusion), kind=kLoop, calls=%fused_computation.4 | loop fusion | flops 12582912 | bytes 100663488 | tf_op jit(solution)/shard_map/jit(_take)/select_n | solution.py:41
  979.3 47.8 %fusion.17 = f32[4,128,32,128]{3,1,0,2:T(8,128)} fusion(f32[32,6,128,4,128]{4,2,3,1,0:T(8,128)} %bitcast.94, bf16[1,32,6,128,128]{4,3,2,1,0:T(8,128)(2,1)} %param.10), kind=kOutput, calls=%fused_computation.22 | convolution fusion | flops 19327352832 | bytes 65011712 | tf_op jit(solution)/shard_map/rjoc,rjcnm->nmro/dot_general | solution.py:45
  1027.1 8.2 copy.38
  1035.3 11.8 copy.54
  1047.1 0.0 all-reduce.5.cloned.1.call-update
  1047.1 170.5 %all-reduce.5.cloned.1.call-done = f32[512,4096]{1,0:T(8,128)} async-done(((f32[512,4096]{1,0:T(8,128)}), f32[512,4096]{1,0:T(8,128)}) %all-reduce.5.cloned.1.call-update) | async-done | bytes 8388624 | tf_op jit(solution)/shard_map/psum | solution.py:50
  1217.6 11.3 sub.7
  (3 shorter events, 0.0 us)
Async XLA Ops:
  111.7 190.3 %all-to-all-start = ((f32[512,32,128]{2,0,1:T(8,128)}), f32[512,32,128]{2,0,1:T(8,128)}, u32[]{:S(2)}, u32[]{:S(2)}) async-start(f32[512,32,128]{2,0,1:T(8,128)} %fusion.8), calls=%async_computation | async-start | bytes 16777216 | tf_op jit(solution)/shard_map/all_to_all | solution.py:38
  302.0 188.8 %all-to-all-start.1 = ((f32[512,32,128]{0,2,1:T(8,128)}), f32[512,32,128]{0,2,1:T(8,128)}, u32[]{:S(2)}, u32[]{:S(2)}) async-start(f32[512,32,128]{0,2,1:T(8,128)} %bitcast.97), calls=%async_computation.1 | async-start | bytes 16777216 | tf_op jit(solution)/shard_map/all_to_all | solution.py:19
  307.0 306.6 %all-reduce.3.cloned.1.call-start = ((), (), s32[]{:S(2)}) async-start(), calls=%async_computation.3 | async-start | bytes 16777216 | tf_op jit(solution)/shard_map/psum | solution.py:50
  440.1 777.6 %all-reduce.5.cloned.1.call-start = ((), (), s32[]{:S(2)}) async-start(), calls=%async_computation.4 | async-start | bytes 16777216 | tf_op jit(solution)/shard_map/psum | solution.py:50
Sparse Core Ops, SparseCore 0:
  440.2 173.3 all-reduce.2
  1047.2 170.3 all-reduce.4
where the time goes:
time: 1250 us; the launch traced here: 1240 us
  waiting for transfers between devices  499 us (40%)
  local copies, waits for them, and re-layouts  206 us (16%)
  blocking collectives  189 us (15%)
  other arithmetic  161 us (13%)
  matrix products  156 us (12%)
  between operations  13.9 us (1%)
    psum x2, waiting for transfers between devices, per_device(): updated = step_scale * lax.psum(summed, 'op') - earlier  273 us
    all_to_all x1, blocking collectives, per_device(): lax.all_to_all(beta_side, 'str', split_axis=1, concat_axis=0, tiled=True)  189 us
    all_to_all x1, waiting for transfers between devices, per_device(): lax.all_to_all(beta_side, 'str', split_axis=1, concat_axis=0, tiled=True)  175 us
    dot_general x2, matrix products, per_device(): jnp.einsum('rjoc,rjcnm->nmro', term_factors, grouped, precision=lax.Preci...  96.1 us
    select_n x3, other arithmetic, per_device(): jnp.take(received.reshape(block_count, block_size, group_count, item_coun...  69.9 us
    select_n x2, other arithmetic, per_device(): jnp.take(current.reshape(row_count, block_count, block_size), column_list...  68.1 us
    dot_general x2, matrix products, per_device(): jnp.einsum('arjc,rjoc->aro', gathered, term_factors, precision=lax.Precis...  60.2 us
    unnamed x6, local copies, waits for them, and re-layouts  53.9 us
  transfers between devices with their start and end apart: 4, of which 4 were waited for; matrix products, arithmetic and copies ran while one was open for 13% of the time, Pallas kernels for 0%

commit v1 on v0

v1 whole, which is shorter than its diff:
```python
import functools
import math

import jax
import jax.numpy as jnp
from jax import lax
from jax.experimental import pallas as pl
from jax.experimental.pallas import tpu as pltpu
from jax.sharding import PartitionSpec as P

STEPS = 2
F32, BF16 = jnp.float32, jnp.bfloat16
VMEM_LIMIT = 60 * 1024 * 1024


def split(x):
    high = x.astype(BF16)
    return high, (x - high.astype(F32)).astype(BF16)


def call(body, grid, in_specs, out_specs, out_shape, scratch, flops, traffic):
    return pl.pallas_call(
        body,
        grid_spec=pltpu.PrefetchScalarGridSpec(
            num_scalar_prefetch=2,
            grid=grid,
            in_specs=in_specs,
            out_specs=out_specs,
            scratch_shapes=scratch,
        ),
        out_shape=out_shape,
        compiler_params=pltpu.CompilerParams(
            dimension_semantics=("arbitrary",), vmem_limit_bytes=VMEM_LIMIT
        ),
        cost_estimate=pl.CostEstimate(flops=flops, bytes_accessed=traffic, transcendentals=0),
    )


def whole(shape):
    return pl.BlockSpec(shape, lambda i, *_: (0,) * len(shape))


def operator_row(value_block, slots):
    return jnp.concatenate([value_block[j] for j in range(slots)], axis=1)


def beta_product(field, values, row, cols_ref, slots):
    left = jnp.concatenate([field[cols_ref[row * slots + j]] for j in range(slots)], axis=1)
    right = operator_row(values, slots)
    both = lax.dot_general(left, right, (((1,), (1,)), ((), ())), preferred_element_type=F32)
    m = both.shape[0] // 2
    return both[:m] + both[m:]


def alpha_product(field, values, row, cols_ref, slots):
    right = jnp.concatenate([field[cols_ref[row * slots + j]] for j in range(slots)], axis=0)
    both = jnp.dot(operator_row(values, slots), right, preferred_element_type=F32)
    n = both.shape[1] // 2
    return both[:, :n] + both[:, n:]


def beta_first(coeffs, previous, values, cols, place, chunk, shards, op_size):
    rows, width = coeffs.shape
    blocks, slots, block, _ = values.shape
    chunks = blocks // shards
    piece = rows // op_size

    def body(cols_ref, place_ref, v_ref, p_ref, a_ref, o_ref, field):
        i = pl.program_id(0)

        @pl.when(i == 0)
        def _():
            for b in range(blocks):
                high, low = split(v_ref[:, b * block : (b + 1) * block])
                field[b, :rows] = high
                field[b, rows:] = low

        o_ref[0, :rows] = beta_product(field, a_ref[0, 0], i * chunks + chunk, cols_ref, slots)
        o_ref[0, rows:] = p_ref[...]

    return call(
        body,
        (shards,),
        [
            whole((rows, width)),
            pl.BlockSpec((piece, block), lambda i, c, q: (q[0], i * chunks + chunk)),
            pl.BlockSpec((1, 1, slots, block, block), lambda i, *_: (i, chunk, 0, 0, 0)),
        ],
        pl.BlockSpec((1, rows + piece, block), lambda i, *_: (i, 0, 0)),
        jax.ShapeDtypeStruct((shards, rows + piece, block), F32),
        [pltpu.VMEM((blocks, 2 * rows, block), BF16)],
        4 * rows * slots * block * block * shards,
        4 * rows * width,
    )(cols, place, coeffs, previous, values.reshape(shards, chunks, slots, block, block))


def alpha_first(received, values, cols, place, scale, op_size):
    shards, deep, block = received.shape
    blocks, slots = values.shape[:2]
    chunks = blocks // shards
    rows = chunks * block
    piece = deep - rows
    group = 4

    def body(cols_ref, place_ref, w_ref, a_ref, o_ref, field):
        i = pl.program_id(0)

        @pl.when(i == 0)
        def _():
            for b in range(blocks):
                at = (b % chunks) * block
                high, low = split(w_ref[b // chunks, at : at + block])
                field[b, :, :block] = high
                field[b, :, block:] = low

        for g in range(group):
            row = i * group + g
            at = pl.multiple_of(lax.rem(row, chunks) * block, block)
            o_ref[lax.div(row, chunks), pl.ds(at, block)] = scale * alpha_product(
                field, a_ref[g], row, cols_ref, slots
            )

        @pl.when(i == blocks // group - 1)
        def _():
            at = pl.multiple_of(place_ref[0] * piece, piece)
            for s in range(shards):
                o_ref[s, pl.ds(at, piece)] = o_ref[s, pl.ds(at, piece)] - w_ref[s, rows:]

    return call(
        body,
        (blocks // group,),
        [
            whole((shards, deep, block)),
            pl.BlockSpec((group, slots, block, block), lambda i, *_: (i, 0, 0, 0)),
        ],
        whole((shards, rows, block)),
        jax.ShapeDtypeStruct((shards, rows, block), F32),
        [pltpu.VMEM((blocks, block, 2 * block), BF16)],
        4 * blocks * slots * block * block * block,
        8 * shards * rows * block,
    )(cols, place, received, values)


def alpha_second(currents, values, cols, place, chunk):
    shards, rows, block = currents[0].shape
    blocks, slots = values.shape[:2]
    chunks = blocks // shards
    wide = chunks * block

    def body(cols_ref, place_ref, *refs):
        v_refs, a_ref, o_ref, field = refs[:chunks], refs[chunks], refs[chunks + 1], refs[chunks + 2]
        i = pl.program_id(0)

        @pl.when(i == 0)
        def _():
            for c in range(chunks):
                for b in range(blocks):
                    at = (b % chunks) * block
                    high, low = split(v_refs[c][b // chunks, at : at + block])
                    field[b, :, c * block : (c + 1) * block] = high
                    field[b, :, wide + c * block : wide + (c + 1) * block] = low

        o_ref[0] = alpha_product(field, a_ref[0, 0], i * chunks + chunk, cols_ref, slots)

    return call(
        body,
        (shards,),
        [whole((shards, rows, block))] * chunks
        + [pl.BlockSpec((1, 1, slots, block, block), lambda i, *_: (i, chunk, 0, 0, 0))],
        pl.BlockSpec((1, block, wide), lambda i, *_: (i, 0, 0)),
        jax.ShapeDtypeStruct((shards, block, wide), F32),
        [pltpu.VMEM((blocks, block, 2 * wide), BF16)],
        4 * shards * slots * block * block * wide,
        4 * shards * rows * wide,
    )(cols, place, *currents, values.reshape(shards, chunks, slots, block, block))


def beta_second(received, coeffs, values, cols, place, scale, chunk, op_size):
    shards, block, wide = received.shape
    blocks, slots = values.shape[:2]
    chunks = blocks // shards
    width = shards * wide
    part = width // op_size
    group = 4

    def body(cols_ref, place_ref, u_ref, v_ref, a_ref, o_ref, field):
        i = pl.program_id(0)

        @pl.when(i == 0)
        def _():
            for b in range(blocks):
                at = (b % chunks) * block
                high, low = split(u_ref[b // chunks, :, at : at + block])
                field[b, :block] = high
                field[b, block:] = low

        for g in range(group):
            row = i * group + g
            o_ref[:, pl.ds(pl.multiple_of(row * block, block), block)] = scale * beta_product(
                field, a_ref[g], row, cols_ref, slots
            )

        @pl.when(i == blocks // group - 1)
        def _():
            at = pl.ds(pl.multiple_of(place_ref[0] * part, part), part)
            o_ref[:, at] = o_ref[:, at] - v_ref[...]

    return call(
        body,
        (blocks // group,),
        [
            whole((shards, block, wide)),
            pl.BlockSpec((block, part), lambda i, c, q: (chunk, q[0])),
            pl.BlockSpec((group, slots, block, block), lambda i, *_: (i, 0, 0, 0)),
        ],
        whole((block, width)),
        jax.ShapeDtypeStruct((block, width), F32),
        [pltpu.VMEM((blocks, 2 * block, block), BF16)],
        4 * blocks * slots * block * block * block,
        8 * width * block,
    )(cols, place, received, coeffs, values)


def per_device(coeffs, previous, block_values, block_cols):
    op_size, shards = lax.axis_size("op"), lax.axis_size("str")
    scale = 2.0 / math.sqrt(block_values.shape[0] * op_size)
    values = block_values[0]
    cols = block_cols[0].reshape(-1)
    place = lax.axis_index("op").astype(jnp.int32).reshape(1)
    chunks = values.shape[0] // shards

    swap = functools.partial(lax.all_to_all, axis_name="str", split_axis=0, concat_axis=0, tiled=True)
    def run(prepare, finish):
        moved, products, sums = [], [], []
        for chunk in range(chunks):
            sent = prepare(chunk)
            if chunk >= 1:
                sent, moved[chunk - 1] = lax.optimization_barrier((sent, moved[chunk - 1]))
            if chunk >= 2:
                product = finish(chunk - 2, moved[chunk - 2])
                sent, product = lax.optimization_barrier((sent, product))
                products.append(product)
            moved.append(swap(sent))
        for chunk in range(len(products), chunks):
            products.append(finish(chunk, moved[chunk]))
        for chunk in range(chunks):
            product = products[chunk]
            if chunk >= 1:
                product, sums[-1] = lax.optimization_barrier((product, sums[-1]))
            sums.append(lax.psum(product, "op"))
        return sums

    currents = run(
        lambda chunk: beta_first(coeffs, previous, values, cols, place, chunk, shards, op_size),
        lambda chunk, arrived: alpha_first(arrived, values, cols, place, scale, op_size),
    )
    outs = run(
        lambda chunk: alpha_second(currents, values, cols, place, chunk),
        lambda chunk, arrived: beta_second(
            arrived, coeffs, values, cols, place, scale, chunk, op_size
        ),
    )
    return jnp.concatenate(outs, axis=0)


def solution(mesh):
    placed = (P("str", None), P("str", None), P("op", None, None, None, None), P("op", None, None))
    return jax.shard_map(
        per_device, mesh=mesh, in_specs=placed, out_specs=P("str", None), check_vma=False
    )
```

time: 1250 us -> 882 us (0.71)
  local copies, waits for them, and re-layouts: 206 us -> 8.54 us
  blocking collectives: 189 us -> 0 us
  Pallas kernels: 0 us -> 184 us
  matrix products: 156 us -> 0 us
  other arithmetic: 161 us -> 5.72 us
  waiting for transfers between devices: 499 us -> 632 us
  starting transfers between devices: 11.4 us -> 34.9 us
    all_to_all x1 -> x0, blocking collectives: 189 us -> none  [per_device(): lax.all_to_all(beta_side, 'str', split_axis=1, concat_axis=0, tiled=True)]
    pallas_call x0 -> x16, Pallas kernels: none -> 184 us  [the longest x4 51.4 us: beta_first(): call(body, (shards,), [whole((rows, width)), pl.BlockSpec((piece, block),...]
    dot_general x4 -> x0, matrix products: 156 us -> none  [the longest x2 96.1 us: per_device(): jnp.einsum('rjoc,rjcnm->nmro', term_factors, grouped, precision=lax.Preci...]
    psum x2 -> x8, waiting for transfers between devices: 273 us -> 422 us  [run(): sums.append(lax.psum(product, 'op'))]
    select_n x5 -> x0, other arithmetic: 138 us -> none  [the longest x3 69.9 us: per_device(): jnp.take(received.reshape(block_count, block_size, group_count, item_coun...]
    gather x4 -> x0, local copies, waits for them, and re-layouts: 88.9 us -> none  [the longest x2 44.4 us: per_device(): jnp.take(current.reshape(row_count, block_count, block_size), column_list...]
    unnamed x6 -> x15, local copies, waits for them, and re-layouts: 53.9 us -> 7.86 us
    all_to_all x2 -> x8, starting transfers between devices: 11.3 us -> 34.4 us  [run(): moved.append(swap(sent))]
  transfers between devices with their start and end apart: 4 -> 16, of which waited for: 4 -> 14; matrix products, arithmetic and copies ran while one was open for 13% -> 0% of each run, Pallas kernels for 0% -> 18%
where the time goes in v1:
time: 882 us; the launch traced here: 879 us
  waiting for transfers between devices  632 us (72%)
  Pallas kernels  184 us (21%)
  starting transfers between devices  34.9 us (4%)
  between operations  13.6 us (2%)
    psum x8, waiting for transfers between devices, run(): sums.append(lax.psum(product, 'op'))  422 us
    all_to_all x8, waiting for transfers between devices, run(): moved.append(swap(sent))  209 us
    pallas_call x4, Pallas kernels, beta_first(): call(body, (shards,), [whole((rows, width)), pl.BlockSpec((piece, block),...  51.4 us
    pallas_call x4, Pallas kernels, alpha_second(): call(body, (shards,), [whole((shards, rows, block))] * chunks + [pl.Block...  49.2 us
    pallas_call x4, Pallas kernels, beta_second(): call(body, (blocks // group,), [whole((shards, block, wide)), pl.BlockSpe...  43.3 us
    pallas_call x4, Pallas kernels, alpha_first(): call(body, (blocks // group,), [whole((shards, deep, block)), pl.BlockSpe...  39.8 us
    all_to_all x8, starting transfers between devices, run(): moved.append(swap(sent))  34.4 us
  transfers between devices with their start and end apart: 16, of which 14 were waited for; matrix products, arithmetic and copies ran while one was open for 0% of the time, Pallas kernels for 18%

profile of v1, /device:TPU:0, one launch (start us, length us, event | category | flops | bytes accessed | tf_op | source)
XLA Modules:
  0.0 878.9 jit_solution(17243014977021742841)
XLA Ops:
  6.5 0.8 copy.5
  7.3 0.7 reshape_squeeze.4.cols_ref
  8.0 12.8 %shard_map.49 = f32[8,640,128]{2,1,0:T(8,128)} custom-call(s32[192]{0:T(256)} %reshape_squeeze.4.cols_ref, s32[1]{0:T(128)} %bitcast.place_ref, f32[512,4096]{1,0:T(8,128)} %v_ref.15, f32[512,4096]{1,0:T(8,128)} %p_ref.7, bf16[8,4,6,128,128]{4,3,2,1,0:T(8,128)(2,1)} %bitcast.3), custom_call_target="tpu_custom_call" | custom-call | flops 1610612736 | bytes 8388608 | tf_op jit(solution)/shard_map/pallas_call | solution.py:81
  20.8 6.4 all-to-all-start
  27.2 12.8 %shard_map.48 = f32[8,640,128]{2,1,0:T(8,128)} custom-call(s32[192]{0:T(256)} %reshape_squeeze.4.cols_ref, s32[1]{0:T(128)} %bitcast.place_ref, f32[512,4096]{1,0:T(8,128)} %v_ref.15, f32[512,4096]{1,0:T(8,128)} %p_ref.7, bf16[8,4,6,128,128]{4,3,2,1,0:T(8,128)(2,1)} %bitcast.4), custom_call_target="tpu_custom_call" | custom-call | flops 1610612736 | bytes 8388608 | tf_op jit(solution)/shard_map/pallas_call | solution.py:81
  40.0 47.5 %all-to-all-done.w_ref = f32[8,640,128]{2,1,0:T(8,128)S(1)} async-done(((f32[8,640,128]{2,1,0:T(8,128)}), f32[8,640,128]{2,1,0:T(8,128)S(1)}, u32[]{:S(2)}, u32[]{:S(2)}) %all-to-all-start) | async-done | bytes 2621472 | tf_op jit(solution)/shard_map/all_to_all | solution.py:243
  87.4 1.5 copy-done.2
  88.9 3.6 all-to-all-start.1
  92.6 12.8 %shard_map.47 = f32[8,640,128]{2,1,0:T(8,128)} custom-call(s32[192]{0:T(256)} %reshape_squeeze.4.cols_ref, s32[1]{0:T(128)} %bitcast.place_ref, f32[512,4096]{1,0:T(8,128)} %v_ref.15, f32[512,4096]{1,0:T(8,128)} %p_ref.7, bf16[8,4,6,128,128]{4,3,2,1,0:T(8,128)(2,1)} %bitcast.5), custom_call_target="tpu_custom_call" | custom-call | flops 1610612736 | bytes 8388608 | tf_op jit(solution)/shard_map/pallas_call | solution.py:81
  105.4 9.9 %shard_map.50 = f32[8,512,128]{2,1,0:T(8,128)} custom-call(s32[192]{0:T(256)} %reshape_squeeze.4.cols_ref, s32[1]{0:T(128)} %bitcast.place_ref, f32[8,640,128]{2,1,0:T(8,128)} %copy-done.2, bf16[32,6,128,128]{3,2,1,0:T(8,128)(2,1)} %bitcast.6), custom_call_target="tpu_custom_call" | custom-call | flops 1610612736 | bytes 4194304 | tf_op jit(solution)/shard_map/pallas_call | solution.py:129
  115.3 37.4 %all-to-all-done.1.w_ref = f32[8,640,128]{2,1,0:T(8,128)S(1)} async-done(((f32[8,640,128]{2,1,0:T(8,128)}), f32[8,640,128]{2,1,0:T(8,128)S(1)}, u32[]{:S(2)}, u32[]{:S(2)}) %all-to-all-start.1) | async-done | bytes 2621472 | tf_op jit(solution)/shard_map/all_to_all | solution.py:243
  152.7 1.5 copy-done.1
  154.2 3.6 all-to-all-start.2
  157.9 0.0 all-reduce.9.cloned.1.call-start
  157.9 0.7 all-reduce.9.cloned.1.call-update
  158.6 12.9 %shard_map.46 = f32[8,640,128]{2,1,0:T(8,128)} custom-call(s32[192]{0:T(256)} %reshape_squeeze.4.cols_ref, s32[1]{0:T(128)} %bitcast.place_ref, f32[512,4096]{1,0:T(8,128)} %v_ref.15, f32[512,4096]{1,0:T(8,128)} %p_ref.7, bf16[8,4,6,128,128]{4,3,2,1,0:T(8,128)(2,1)} %bitcast.7), custom_call_target="tpu_custom_call" | custom-call | flops 1610612736 | bytes 8388608 | tf_op jit(solution)/shard_map/pallas_call | solution.py:81
  171.5 10.0 %shard_map.51 = f32[8,512,128]{2,1,0:T(8,128)} custom-call(s32[192]{0:T(256)} %reshape_squeeze.4.cols_ref, s32[1]{0:T(128)} %bitcast.place_ref, f32[8,640,128]{2,1,0:T(8,128)} %copy-done.1, bf16[32,6,128,128]{3,2,1,0:T(8,128)(2,1)} %bitcast.8), custom_call_target="tpu_custom_call" | custom-call | flops 1610612736 | bytes 4194304 | tf_op jit(solution)/shard_map/pallas_call | solution.py:129
  181.5 36.6 %all-to-all-done.2.w_ref = f32[8,640,128]{2,1,0:T(8,128)S(1)} async-done(((f32[8,640,128]{2,1,0:T(8,128)}), f32[8,640,128]{2,1,0:T(8,128)S(1)}, u32[]{:S(2)}, u32[]{:S(2)}) %all-to-all-start.2) | async-done | bytes 2621472 | tf_op jit(solution)/shard_map/all_to_all | solution.py:243
  218.1 1.5 copy-done
  219.6 4.4 all-to-all-start.3
  224.0 0.0 all-reduce.11.cloned.1.call-start
  224.0 8.7 all-reduce.9.cloned.1.call-done.refs_0_
  232.7 0.0 all-reduce.11.cloned.1.call-update
  232.7 0.0 all-reduce.13.cloned.1.call-start
  232.8 9.9 %shard_map.52 = f32[8,512,128]{2,1,0:T(8,128)} custom-call(s32[192]{0:T(256)} %reshape_squeeze.4.cols_ref, s32[1]{0:T(128)} %bitcast.place_ref, f32[8,640,128]{2,1,0:T(8,128)} %copy-done, bf16[32,6,128,128]{3,2,1,0:T(8,128)(2,1)} %bitcast.9), custom_call_target="tpu_custom_call" | custom-call | flops 1610612736 | bytes 4194304 | tf_op jit(solution)/shard_map/pallas_call | solution.py:129
  242.7 62.6 %all-reduce.11.cloned.1.call-done.refs_1_ = f32[8,512,128]{2,1,0:T(8,128)} async-done(((f32[8,512,128]{2,1,0:T(8,128)}), f32[8,512,128]{2,1,0:T(8,128)}) %all-reduce.11.cloned.1.call-update) | async-done | bytes 2097168 | tf_op jit(solution)/shard_map/psum | solution.py:250
  305.3 0.0 all-reduce.13.cloned.1.call-update
  305.3 0.2 all-reduce.15.cloned.1.call-start
  305.5 0.0 all-to-all-done.3.w_ref
  305.6 10.0 %shard_map.53 = f32[8,512,128]{2,1,0:T(8,128)} custom-call(s32[192]{0:T(256)} %reshape_squeeze.4.cols_ref, s32[1]{0:T(128)} %bitcast.place_ref, f32[8,640,128]{2,1,0:T(8,128)} %all-to-all-done.3.w_ref, bf16[32,6,128,128]{3,2,1,0:T(8,128)(2,1)} %bitcast.10), custom_call_target="tpu_custom_call" | custom-call | flops 1610612736 | bytes 4194304 | tf_op jit(solution)/shard_map/pallas_call | solution.py:129
  315.5 62.4 %all-reduce.13.cloned.1.call-done.refs_2_ = f32[8,512,128]{2,1,0:T(8,128)} async-done(((f32[8,512,128]{2,1,0:T(8,128)}), f32[8,512,128]{2,1,0:T(8,128)}) %all-reduce.13.cloned.1.call-update) | async-done | bytes 2097168 | tf_op jit(solution)/shard_map/psum | solution.py:250
  377.9 0.0 all-reduce.15.cloned.1.call-update
  378.0 72.4 %all-reduce.15.cloned.1.call-done.refs_3_ = f32[8,512,128]{2,1,0:T(8,128)} async-done(((f32[8,512,128]{2,1,0:T(8,128)}), f32[8,512,128]{2,1,0:T(8,128)}) %all-reduce.15.cloned.1.call-update) | async-done | bytes 2097168 | tf_op jit(solution)/shard_map/psum | solution.py:250
  450.4 12.3 %shard_map.57 = f32[8,128,512]{2,1,0:T(8,128)} custom-call(s32[192]{0:T(256)} %reshape_squeeze.4.cols_ref, s32[1]{0:T(128)} %bitcast.place_ref, f32[8,512,128]{2,1,0:T(8,128)} %all-reduce.9.cloned.1.call-done.refs_0_, f32[8,512,128]{2,1,0:T(8,128)} %all-reduce.11.cloned.1.call-done.refs_1_, f32[8,512,128]{2,1,0:T(8,128)} %all-reduce.13.cloned.1.call-done.refs_2_, ...), custom_call_target="tpu_custom_call" | custom-call | flops 1610612736 | bytes 8388608 | tf_op jit(solution)/shard_map/pallas_call | solution.py:165
  462.7 4.6 all-to-all-start.4
  467.3 12.3 %shard_map.56 = f32[8,128,512]{2,1,0:T(8,128)} custom-call(s32[192]{0:T(256)} %reshape_squeeze.4.cols_ref, s32[1]{0:T(128)} %bitcast.place_ref, f32[8,512,128]{2,1,0:T(8,128)} %all-reduce.9.cloned.1.call-done.refs_0_, f32[8,512,128]{2,1,0:T(8,128)} %all-reduce.11.cloned.1.call-done.refs_1_, f32[8,512,128]{2,1,0:T(8,128)} %all-reduce.13.cloned.1.call-done.refs_2_, ...), custom_call_target="tpu_custom_call" | custom-call | flops 1610612736 | bytes 8388608 | tf_op jit(solution)/shard_map/pallas_call | solution.py:165
  479.6 36.7 %all-to-all-done.4.u_ref = f32[8,128,512]{2,1,0:T(8,128)S(1)} async-done(((f32[8,128,512]{2,1,0:T(8,128)}), f32[8,128,512]{2,1,0:T(8,128)S(1)}, u32[]{:S(2)}, u32[]{:S(2)}) %all-to-all-start.4) | async-done | bytes 2097184 | tf_op jit(solution)/shard_map/all_to_all | solution.py:243
  516.3 1.3 copy-done.5
  517.6 3.6 all-to-all-start.5
  521.3 12.3 %shard_map.55 = f32[8,128,512]{2,1,0:T(8,128)} custom-call(s32[192]{0:T(256)} %reshape_squeeze.4.cols_ref, s32[1]{0:T(128)} %bitcast.place_ref, f32[8,512,128]{2,1,0:T(8,128)} %all-reduce.9.cloned.1.call-done.refs_0_, f32[8,512,128]{2,1,0:T(8,128)} %all-reduce.11.cloned.1.call-done.refs_1_, f32[8,512,128]{2,1,0:T(8,128)} %all-reduce.13.cloned.1.call-done.refs_2_, ...), custom_call_target="tpu_custom_call" | custom-call | flops 1610612736 | bytes 8388608 | tf_op jit(solution)/shard_map/pallas_call | solution.py:165
  533.6 10.7 %shard_map.58 = f32[128,4096]{1,0:T(8,128)} custom-call(s32[192]{0:T(256)} %reshape_squeeze.4.cols_ref, s32[1]{0:T(128)} %bitcast.place_ref, f32[8,128,512]{2,1,0:T(8,128)} %copy-done.5, f32[512,4096]{1,0:T(8,128)} %v_ref.15, bf16[32,6,128,128]{3,2,1,0:T(8,128)(2,1)} %bitcast.14), custom_call_target="tpu_custom_call" | custom-call | flops 1610612736 | bytes 4194304 | tf_op jit(solution)/shard_map/pallas_call | solution.py:208
  544.3 25.9 %all-to-all-done.5.u_ref = f32[8,128,512]{2,1,0:T(8,128)S(1)} async-done(((f32[8,128,512]{2,1,0:T(8,128)}), f32[8,128,512]{2,1,0:T(8,128)S(1)}, u32[]{:S(2)}, u32[]{:S(2)}) %all-to-all-start.5) | async-done | bytes 2097184 | tf_op jit(solution)/shard_map/all_to_all | solution.py:243
  570.2 1.3 copy-done.4
  571.5 3.6 all-to-all-start.6
  575.1 0.0 all-reduce.17.cloned.1.call-start
  575.2 0.5 all-reduce.17.cloned.1.call-update
  575.7 0.0 all-reduce.19.cloned.1.call-start
  575.8 12.3 %shard_map.54 = f32[8,128,512]{2,1,0:T(8,128)} custom-call(s32[192]{0:T(256)} %reshape_squeeze.4.cols_ref, s32[1]{0:T(128)} %bitcast.place_ref, f32[8,512,128]{2,1,0:T(8,128)} %all-reduce.9.cloned.1.call-done.refs_0_, f32[8,512,128]{2,1,0:T(8,128)} %all-reduce.11.cloned.1.call-done.refs_1_, f32[8,512,128]{2,1,0:T(8,128)} %all-reduce.13.cloned.1.call-done.refs_2_, ...), custom_call_target="tpu_custom_call" | custom-call | flops 1610612736 | bytes 8388608 | tf_op jit(solution)/shard_map/pallas_call | solution.py:165
  588.1 10.7 %shard_map.59 = f32[128,4096]{1,0:T(8,128)} custom-call(s32[192]{0:T(256)} %reshape_squeeze.4.cols_ref, s32[1]{0:T(128)} %bitcast.place_ref, f32[8,128,512]{2,1,0:T(8,128)} %copy-done.4, f32[512,4096]{1,0:T(8,128)} %v_ref.15, bf16[32,6,128,128]{3,2,1,0:T(8,128)(2,1)} %bitcast.16), custom_call_target="tpu_custom_call" | custom-call | flops 1610612736 | bytes 4194304 | tf_op jit(solution)/shard_map/pallas_call | solution.py:208
  598.9 25.2 %all-to-all-done.6.u_ref = f32[8,128,512]{2,1,0:T(8,128)S(1)} async-done(((f32[8,128,512]{2,1,0:T(8,128)}), f32[8,128,512]{2,1,0:T(8,128)S(1)}, u32[]{:S(2)}, u32[]{:S(2)}) %all-to-all-start.6) | async-done | bytes 2097184 | tf_op jit(solution)/shard_map/all_to_all | solution.py:243
  624.1 24.6 %all-reduce.17.cloned.1.call-done = f32[128,4096]{1,0:T(8,128)} async-done(((f32[128,4096]{1,0:T(8,128)}), f32[128,4096]{1,0:T(8,128)}) %all-reduce.17.cloned.1.call-update) | async-done | bytes 2097168 | tf_op jit(solution)/shard_map/psum | solution.py:250
  648.7 0.0 all-reduce.19.cloned.1.call-update
  648.7 4.6 all-to-all-start.7
  653.3 0.0 all-reduce.21.cloned.1.call-start
  653.4 10.9 %shard_map.60 = f32[128,4096]{1,0:T(8,128)} custom-call(s32[192]{0:T(256)} %reshape_squeeze.4.cols_ref, s32[1]{0:T(128)} %bitcast.place_ref, f32[8,128,512]{2,1,0:T(8,128)} %copy-done.3, f32[512,4096]{1,0:T(8,128)} %v_ref.15, bf16[32,6,128,128]{3,2,1,0:T(8,128)(2,1)} %bitcast.17), custom_call_target="tpu_custom_call" | custom-call | flops 1610612736 | bytes 4194304 | tf_op jit(solution)/shard_map/pallas_call | solution.py:208
  664.2 56.9 %all-reduce.19.cloned.1.call-done = f32[128,4096]{1,0:T(8,128)} async-done(((f32[128,4096]{1,0:T(8,128)}), f32[128,4096]{1,0:T(8,128)}) %all-reduce.19.cloned.1.call-update) | async-done | bytes 2097168 | tf_op jit(solution)/shard_map/psum | solution.py:250
  721.1 0.0 all-reduce.21.cloned.1.call-update
  721.2 0.0 all-reduce.23.cloned.1.call-start
  721.2 0.0 all-to-all-done.7.u_ref
  721.2 10.9 %shard_map.61 = f32[128,4096]{1,0:T(8,128)} custom-call(s32[192]{0:T(256)} %reshape_squeeze.4.cols_ref, s32[1]{0:T(128)} %bitcast.place_ref, f32[8,128,512]{2,1,0:T(8,128)} %all-to-all-done.7.u_ref, f32[512,4096]{1,0:T(8,128)} %v_ref.15, bf16[32,6,128,128]{3,2,1,0:T(8,128)(2,1)} %bitcast.18), custom_call_target="tpu_custom_call" | custom-call | flops 1610612736 | bytes 4194304 | tf_op jit(solution)/shard_map/pallas_call | solution.py:208
  732.2 61.6 %all-reduce.21.cloned.1.call-done = f32[128,4096]{1,0:T(8,128)} async-done(((f32[128,4096]{1,0:T(8,128)}), f32[128,4096]{1,0:T(8,128)}) %all-reduce.21.cloned.1.call-update) | async-done | bytes 2097168 | tf_op jit(solution)/shard_map/psum | solution.py:250
  793.8 0.0 all-reduce.23.cloned.1.call-update
  793.8 72.6 %all-reduce.23.cloned.1.call-done = f32[128,4096]{1,0:T(8,128)} async-done(((f32[128,4096]{1,0:T(8,128)}), f32[128,4096]{1,0:T(8,128)}) %all-reduce.23.cloned.1.call-update) | async-done | bytes 2097168 | tf_op jit(solution)/shard_map/psum | solution.py:250
  866.4 5.7 pad_maximum_fusion
  (9 shorter events, 0.0 us)
Async XLA Ops:
  20.8 66.6 %all-to-all-start = ((f32[8,640,128]{2,1,0:T(8,128)}), f32[8,640,128]{2,1,0:T(8,128)S(1)}, u32[]{:S(2)}, u32[]{:S(2)}) async-start(f32[8,640,128]{2,1,0:T(8,128)} %shard_map.49), calls=%async_computation | async-start | bytes 5242880 | tf_op jit(solution)/shard_map/all_to_all | solution.py:243
  87.4 1.5 copy-start.2
  88.9 63.8 %all-to-all-start.1 = ((f32[8,640,128]{2,1,0:T(8,128)}), f32[8,640,128]{2,1,0:T(8,128)S(1)}, u32[]{:S(2)}, u32[]{:S(2)}) async-start(f32[8,640,128]{2,1,0:T(8,128)} %shard_map.48), calls=%async_computation.1 | async-start | bytes 5242880 | tf_op jit(solution)/shard_map/all_to_all | solution.py:243
  152.7 1.5 copy-start.1
  154.2 63.8 %all-to-all-start.2 = ((f32[8,640,128]{2,1,0:T(8,128)}), f32[8,640,128]{2,1,0:T(8,128)S(1)}, u32[]{:S(2)}, u32[]{:S(2)}) async-start(f32[8,640,128]{2,1,0:T(8,128)} %shard_map.47), calls=%async_computation.2 | async-start | bytes 5242880 | tf_op jit(solution)/shard_map/all_to_all | solution.py:243
  157.9 74.8 %all-reduce.9.cloned.1.call-start = ((), (), s32[]{:S(2)}) async-start(), calls=%async_computation.8 | async-start | bytes 4194304 | tf_op jit(solution)/shard_map/psum | solution.py:250
  218.1 1.5 copy-start
  219.6 86.0 %all-to-all-start.3 = ((f32[8,640,128]{2,1,0:T(8,128)}), f32[8,640,128]{2,1,0:T(8,128)}, u32[]{:S(2)}, u32[]{:S(2)}) async-start(f32[8,640,128]{2,1,0:T(8,128)} %shard_map.46), calls=%async_computation.3 | async-start | bytes 5242880 | tf_op jit(solution)/shard_map/all_to_all | solution.py:243
  224.0 81.3 %all-reduce.11.cloned.1.call-start = ((), (), s32[]{:S(2)}) async-start(), calls=%async_computation.9 | async-start | bytes 4194304 | tf_op jit(solution)/shard_map/psum | solution.py:250
  232.7 145.2 %all-reduce.13.cloned.1.call-start = ((), (), s32[]{:S(2)}) async-start(), calls=%async_computation.10 | async-start | bytes 4194304 | tf_op jit(solution)/shard_map/psum | solution.py:250
  305.3 145.1 %all-reduce.15.cloned.1.call-start = ((), (), s32[]{:S(2)}) async-start(), calls=%async_computation.11 | async-start | bytes 4194304 | tf_op jit(solution)/shard_map/psum | solution.py:250
  462.7 53.6 %all-to-all-start.4 = ((f32[8,128,512]{2,1,0:T(8,128)}), f32[8,128,512]{2,1,0:T(8,128)S(1)}, u32[]{:S(2)}, u32[]{:S(2)}) async-start(f32[8,128,512]{2,1,0:T(8,128)} %shard_map.57), calls=%async_computation.4 | async-start | bytes 4194304 | tf_op jit(solution)/shard_map/all_to_all | solution.py:243
  516.3 1.3 copy-start.5
  517.6 52.6 %all-to-all-start.5 = ((f32[8,128,512]{2,1,0:T(8,128)}), f32[8,128,512]{2,1,0:T(8,128)S(1)}, u32[]{:S(2)}, u32[]{:S(2)}) async-start(f32[8,128,512]{2,1,0:T(8,128)} %shard_map.56), calls=%async_computation.5 | async-start | bytes 4194304 | tf_op jit(solution)/shard_map/all_to_all | solution.py:243
  570.2 1.3 copy-start.4
  571.5 52.6 %all-to-all-start.6 = ((f32[8,128,512]{2,1,0:T(8,128)}), f32[8,128,512]{2,1,0:T(8,128)S(1)}, u32[]{:S(2)}, u32[]{:S(2)}) async-start(f32[8,128,512]{2,1,0:T(8,128)} %shard_map.55), calls=%async_computation.6 | async-start | bytes 4194304 | tf_op jit(solution)/shard_map/all_to_all | solution.py:243
  575.1 73.5 %all-reduce.17.cloned.1.call-start = ((), (), s32[]{:S(2)}) async-start(), calls=%async_computation.12 | async-start | bytes 4194304 | tf_op jit(solution)/shard_map/psum | solution.py:250
  575.7 145.4 %all-reduce.19.cloned.1.call-start = ((), (), s32[]{:S(2)}) async-start(), calls=%async_computation.13 | async-start | bytes 4194304 | tf_op jit(solution)/shard_map/psum | solution.py:250
  624.1 24.6 %copy-start.3 = (f32[8,128,512]{2,1,0:T(8,128)}, f32[8,128,512]{2,1,0:T(8,128)S(1)}, u32[]{:S(2)}) copy-start(f32[8,128,512]{2,1,0:T(8,128)S(1)} %all-to-all-done.6.u_ref) | copy-start | bytes 6291460
  648.7 72.5 %all-to-all-start.7 = ((f32[8,128,512]{2,1,0:T(8,128)}), f32[8,128,512]{2,1,0:T(8,128)}, u32[]{:S(2)}, u32[]{:S(2)}) async-start(f32[8,128,512]{2,1,0:T(8,128)} %shard_map.54), calls=%async_computation.7 | async-start | bytes 4194304 | tf_op jit(solution)/shard_map/all_to_all | solution.py:243
  653.3 140.4 %all-reduce.21.cloned.1.call-start = ((), (), s32[]{:S(2)}) async-start(), calls=%async_computation.14 | async-start | bytes 4194304 | tf_op jit(solution)/shard_map/psum | solution.py:250
  721.2 145.2 %all-reduce.23.cloned.1.call-start = ((), (), s32[]{:S(2)}) async-start(), calls=%async_computation.15 | async-start | bytes 4194304 | tf_op jit(solution)/shard_map/psum | solution.py:250
  732.2 134.2 %copy-start.6 = (f32[128,4096]{1,0:T(8,128)S(1)}, f32[128,4096]{1,0:T(8,128)}, u32[]{:S(2)}) copy-start(f32[128,4096]{1,0:T(8,128)} %all-reduce.17.cloned.1.call-done) | copy-start | bytes 6291460
Sparse Core Ops, SparseCore 0:
  161.8 70.8 all-reduce.8
  235.8 69.4 all-reduce.10
  308.4 69.4 all-reduce.12
  380.9 69.4 all-reduce.14
  578.7 69.8 all-reduce.16
  651.6 69.4 all-reduce.18
  724.2 69.4 all-reduce.20
  796.9 69.4 all-reduce.22
